TPU v7x, 256 devices: a whole 4x4x8 slice. The times are simulated.
256 devices in a mesh: grid: 8 (over y, core), wide: 32 (over z, x).
Axes of the slice: x: 4, y: 4, z: 8, core: 2. Of those that a mesh axis runs over, the one named last changes fastest.
Arguments:
- values: bfloat16 [3584, 64, 4096], P(('grid', 'wide')), may hold values from 0 to 1
- a_block: int32 [3584], P(('grid', 'wide')), may hold values from 0 to 63, as said below
- b_block: int32 [3584], P(('grid', 'wide')), may hold values from 0 to 15
- c_block: int32 [3584], P(('grid', 'wide')), may hold values from 0 to 63
- held: int32 [3584], P(('grid', 'wide')), may hold values from 0 to 1, as said below
- factor_a: bfloat16 [32768, 256], P(('grid', 'wide')), may hold values from -6 to 6
- factor_b: bfloat16 [32768, 256], P(('wide', 'grid')), may hold values from -2.390625 to 2.390625
- factor_c: bfloat16 [4096, 256], replicated, may hold values from -2.390625 to 2.390625
Outputs:
- next_a: float32 [32768, 256], P(('grid', 'wide'))
- next_b: float32 [32768, 256], P(('wide', 'grid'))
- held_loss: float32 [], replicated
Inputs may be any that keep to these rules, and one draw needn't show every extreme that they name: Among the blocks of one device, at most 1 have a_block values with the same a_block // 2; on some device some such value is shared by exactly 1 block. Every device holds 1 to 3 held-out blocks; some device holds exactly 3.
All inputs are finite; a program needn't handle non-finite values.
Results may differ from a plain program's by a relative error of at most 0.0011.
Values may be sent and summed in bfloat16 or wider, within the bound.
No kernel may reach another device: no remote copies, remote signals or barrier semaphores. Data moves between devices by JAX's collectives and lax.ppermute only.
A program may use at most 64 MiB of HBM per device.

v0:
```python
import jax
import jax.numpy as jnp
from jax import lax
from jax.sharding import PartitionSpec as P

step_size = 0.05


def block_terms(inputs):
    entries, a_rows, b_rows, c_rows, flag = inputs
    side = a_rows.shape[0]
    width = a_rows.shape[1]
    khatri = (
        b_rows.astype(jnp.float32)[:, None, :] * c_rows.astype(jnp.float32)[None, :, :]
    ).astype(jnp.bfloat16)
    khatri = khatri.reshape(side * side, width)
    model = lax.dot_general(
        a_rows, khatri, (((1,), (1,)), ((), ())), preferred_element_type=jnp.float32
    )
    entry_f = entries.astype(jnp.float32)
    resid = ((jax.nn.sigmoid(model) - entry_f) * (1.0 - flag)).astype(jnp.bfloat16)
    loss_part = jnp.sum(jax.nn.softplus(model) - entry_f * model) * flag
    grad_rows = jnp.dot(resid, khatri, preferred_element_type=jnp.float32)
    partial_sum = lax.dot_general(
        resid, a_rows, (((0,), (0,)), ((), ())), preferred_element_type=jnp.float32
    )
    grad_cols = jnp.sum(
        partial_sum.reshape(side, side, width) * c_rows.astype(jnp.float32)[None, :, :], axis=1
    )
    return (grad_rows, grad_cols, loss_part)


def per_device(values, a_block, b_block, c_block, held, factor_a, factor_b, factor_c):
    blocks = values.shape[0]
    side = values.shape[1]
    width = factor_a.shape[1]
    highest = lax.Precision.HIGHEST
    own_blocks = factor_a.shape[0] // side
    wide_count = lax.axis_size("wide")
    b_panel = lax.all_gather(factor_b, "grid", axis=0, tiled=True)
    b_rows = b_panel.reshape(-1, side, width)[b_block]
    c_rows = factor_c.reshape(-1, side, width)[c_block]
    a_panel = lax.all_gather(factor_a, "wide", axis=0, tiled=True)
    a_rows = a_panel.reshape(-1, side, width)[a_block]
    flags = held.astype(jnp.float32)
    grad_rows, grad_cols, loss_parts = lax.map(block_terms, (values, a_rows, b_rows, c_rows, flags))
    panel_blocks = own_blocks * wide_count
    matches = (a_block[:, None] == jnp.arange(panel_blocks)[None, :]).astype(jnp.float32)
    panel_grad = jnp.einsum("np,nk->pk", matches, grad_rows.reshape(blocks, -1), precision=highest)
    grad_a = lax.psum_scatter(
        panel_grad.reshape(panel_blocks * side, width), "wide", scatter_dimension=0, tiled=True
    )
    b_panel_blocks = b_panel.shape[0] // side
    b_matches = (b_block[:, None] == jnp.arange(b_panel_blocks)[None, :]).astype(jnp.float32)
    b_panel_grad = jnp.einsum(
        "np,nk->pk", b_matches, grad_cols.reshape(blocks, -1), precision=highest
    )
    grad_b = lax.psum_scatter(
        b_panel_grad.reshape(b_panel_blocks * side, width), "grid", scatter_dimension=0, tiled=True
    )
    loss_total, held_total = lax.psum((jnp.sum(loss_parts), jnp.sum(flags)), ("grid", "wide"))
    held_loss = loss_total / (held_total * (side * side * side))
    next_a = factor_a.astype(jnp.float32) - step_size * grad_a
    next_b = factor_b.astype(jnp.float32) - step_size * grad_b
    return (next_a, next_b, held_loss)


def solution(mesh):
    in_specs = (
        P(("grid", "wide"), None, None),
        P(("grid", "wide")),
        P(("grid", "wide")),
        P(("grid", "wide")),
        P(("grid", "wide")),
        P(("grid", "wide"), None),
        P(("wide", "grid"), None),
        P(),
    )
    out_specs = (P(("grid", "wide"), None), P(("wide", "grid"), None), P())
    return jax.shard_map(
        per_device, mesh=mesh, in_specs=in_specs, out_specs=out_specs, check_vma=False
    )
```

profile of v0, /device:TPU:8, one launch (start us, length us, event | category | flops | bytes accessed | tf_op | source)
XLA Modules:
  0.0 559.0 jit_solution(8834478500784365606)
XLA Ops:
  10.6 13.5 %all_gather.7 = bf16[1024,256]{1,0:T(8,128)(2,1)S(1)} all-gather(bf16[128,256]{1,0:T(8,128)(2,1)} %param.16), channel_id=1, replica_groups=mesh['grid'=8,'wide'=32] {'grid'}, dimensions={0}, use_global_device_ids=true | all-gather | bytes 589824 | tf_op jit(solution)/shard_map/all_gather | solution.py:40
  25.5 66.0 %all-gather.2.cloned.1.call-done = bf16[4096,256]{1,0:T(8,128)(2,1)} async-done(((bf16[128,256]{1,0:T(8,128)(2,1)}), bf16[4096,256]{1,0:T(8,128)(2,1)}) %all-gather.2.cloned.1.call-update) | async-done | bytes 2097168 | tf_op jit(solution)/shard_map/all_gather | solution.py:43
  91.5 2.9 gather_fusion
  94.4 195.9 %while.14 = (s32[]{:T(128)}, f32[14,64,256]{2,1,0:T(8,128)}, f32[14,64,256]{2,1,0:T(8,128)}, f32[14]{0:T(128)S(1)}, bf16[14,64,256]{2,1,0:T(8,128)(2,1)}, /*inde...) while((s32[]{:T(128)}, f32[14,64,256]{2,1,0:T(8,128)}, ...), condition=%wide.region_3.4_spmd, body=%wide.region_0.3_spmd.sunk | while | flops 411058176 | bytes 19072724 | solution.py:46
  97.1 3.3 fusion.34
  101.7 2.7 fusion.35
  105.9 1.9 multiply_reduce_fusion.2
  111.1 3.3 fusion.34
  115.7 2.7 fusion.35
  119.8 1.9 multiply_reduce_fusion.2
  125.1 3.3 fusion.34
  129.7 2.7 fusion.35
  139.1 3.3 fusion.34
  143.7 2.7 fusion.35
  147.8 1.9 multiply_reduce_fusion.2
  153.1 3.3 fusion.34
  157.7 2.7 fusion.35
  161.8 1.9 multiply_reduce_fusion.2
  167.1 3.3 fusion.34
  171.7 2.7 fusion.35
  175.8 1.9 multiply_reduce_fusion.2
  181.1 3.3 fusion.34
  185.7 2.7 fusion.35
  195.1 3.3 fusion.34
  199.7 2.7 fusion.35
  203.8 1.9 multiply_reduce_fusion.2
  209.0 3.3 fusion.34
  213.7 2.7 fusion.35
  217.8 1.9 multiply_reduce_fusion.2
  223.0 3.3 fusion.34
  227.6 2.7 fusion.35
  231.7 1.9 multiply_reduce_fusion.2
  237.0 3.3 fusion.34
  241.6 2.7 fusion.35
  245.7 1.9 multiply_reduce_fusion.2
  251.0 3.3 fusion.34
  255.6 2.7 fusion.35
  259.7 1.9 multiply_reduce_fusion.2
  265.0 3.3 fusion.34
  269.6 2.7 fusion.35
  273.7 1.9 multiply_reduce_fusion.2
  279.0 3.3 fusion.34
  283.6 2.7 fusion.35
  287.7 1.9 multiply_reduce_fusion.2
  296.1 3.9 fusion.12
  300.0 4.9 reshape.59
  306.8 73.6 %all-reduce = (f32[]{:T(128)}, f32[]{:T(128)}) all-reduce(f32[]{:T(128)} %reduce_sum.36, f32[]{:T(128)} %convert_reduce_fusion), channel_id=1, replica_groups=mesh['grid'=8,'wide'=32] {'grid','wide'}, use_global_device_ids=true, to_apply=%region_7.8 | all-reduce | flops 2 | bytes 16 | tf_op jit(solution)/shard_map/psum | solution.py:61
  383.3 166.5 %reduce-scatter.3.cloned.1.call-done = f32[128,256]{1,0:T(8,128)} async-done(((f32[4096,256]{1,0:T(8,128)}), f32[128,256]{1,0:T(8,128)}) %reduce-scatter.3.cloned.1.call-update) | async-done | bytes 131088 | tf_op jit(solution)/shard_map/reduce_scatter | solution.py:50
  (155 shorter events, 76.9 us)
Async XLA Ops:
  7.2 2.2 copy-start
  7.2 18.3 %copy-start.5 = (s32[14]{0:T(128)S(1)}, s32[14]{0:T(128)}, u32[]{:S(2)}) copy-start(s32[14]{0:T(128)} %param.11) | copy-start | bytes 172
  7.2 84.3 %all-gather.2.cloned.1.call-start = ((), (), s32[]{:S(2)}) async-start(), calls=%async_computation.2 | async-start | bytes 2162688 | tf_op jit(solution)/shard_map/all_gather | solution.py:43
  7.9 373.8 %reduce-scatter.5.cloned.1.call-start = ((), (), s32[]{:S(2)}) async-start(), calls=%async_computation.4 | async-start | bytes 1179648 | tf_op jit(solution)/shard_map/reduce_scatter | solution.py:58
  97.1 3.3 copy-start.1
  111.1 3.3 copy-start.1
  125.1 3.3 copy-start.1
  139.1 3.3 copy-start.1
  153.1 3.3 copy-start.1
  167.1 3.3 copy-start.1
  181.1 3.3 copy-start.1
  195.0 3.3 copy-start.1
  209.0 3.3 copy-start.1
  223.0 3.3 copy-start.1
  237.0 3.3 copy-start.1
  251.0 3.3 copy-start.1
  265.0 3.3 copy-start.1
  279.0 3.3 copy-start.1
  290.3 1.9 copy-start.4
  294.2 255.6 %reduce-scatter.3.cloned.1.call-start = ((), (), s32[]{:S(2)}) async-start(), calls=%async_computation.3 | async-start | bytes 4325376 | tf_op jit(solution)/shard_map/reduce_scatter | solution.py:50
  304.9 0.7 copy-start.6
  304.9 76.8 %copy-start.2 = (bf16[128,256]{1,0:T(8,128)(2,1)S(1)}, bf16[128,256]{1,0:T(8,128)(2,1)}, u32[]{:S(2)}) copy-start(bf16[128,256]{1,0:T(8,128)(2,1)} %param.16) | copy-start | bytes 196612
  304.9 244.9 %copy-start.3 = (bf16[128,256]{1,0:T(8,128)(2,1)S(1)}, bf16[128,256]{1,0:T(8,128)(2,1)}, u32[]{:S(2)}) copy-start(bf16[128,256]{1,0:T(8,128)(2,1)} %param.15) | copy-start | bytes 196612
Sparse Core Ops, SparseCore 0:
  10.6 80.8 all-gather.1
  294.3 28.5 reduce-scatter.4
  326.8 222.9 reduce-scatter.2
where the time goes:
time: 562 us; the launch traced here: 559 us
  waiting for transfers between devices  233 us (41%)
  matrix products  115 us (20%)
  blocking collectives  87.2 us (16%)
  local copies, waits for them, and re-layouts  52.6 us (9%)
  loops' own time  27.7 us (5%)
  other arithmetic  26.8 us (5%)
  between operations  16.3 us (3%)
    reduce_scatter x1, waiting for transfers between devices, per_device(): lax.psum_scatter(panel_grad.reshape(panel_blocks * side, width), 'wide',...  166 us
    psum x1, blocking collectives, per_device(): lax.psum((jnp.sum(loss_parts), jnp.sum(flags)), ('grid', 'wide'))  73.6 us
    all_gather x1, waiting for transfers between devices, per_device(): a_panel = lax.all_gather(factor_a, 'wide', axis=0, tiled=True)  66 us
    dot_general x14, matrix products, block_terms(): lax.dot_general(a_rows, khatri, (((1,), (1,)), ((), ())), preferred_eleme...  46.2 us
    dot_general x14, matrix products, block_terms(): grad_rows = jnp.dot(resid, khatri, preferred_element_type=jnp.float32)  37.5 us
    another operation x1, loops' own time, per_device(): lax.map(block_terms, (values, a_rows, b_rows, c_rows, flags))  27.7 us
    dot_general x14, matrix products, block_terms(): lax.dot_general(resid, a_rows, (((0,), (0,)), ((), ())), preferred_elemen...  26.9 us
    dot_general x14, local copies, waits for them, and re-layouts, block_terms(): lax.dot_general(resid, a_rows, (((0,), (0,)), ((), ())), preferred_elemen...  18.7 us
  transfers between devices with their start and end apart: 3, of which 2 were waited for; matrix products, arithmetic and copies ran while one was open for 3% of the time, Pallas kernels for 0%

commit v1 on v0

--- a/solution.py
+++ b/solution.py
@@ -40,7 +40,15 @@
     b_panel = lax.all_gather(factor_b, "grid", axis=0, tiled=True)
     b_rows = b_panel.reshape(-1, side, width)[b_block]
     c_rows = factor_c.reshape(-1, side, width)[c_block]
-    a_panel = lax.all_gather(factor_a, "wide", axis=0, tiled=True)
+    a_panel = jnp.concatenate(
+        jax.lax.all_to_all(
+            jnp.stack(jax.lax.axis_size("wide") * [factor_a]),
+            split_axis=0,
+            concat_axis=0,
+            axis_name="wide",
+        ),
+        axis=0,
+    )
     a_rows = a_panel.reshape(-1, side, width)[a_block]
     flags = held.astype(jnp.float32)
     grad_rows, grad_cols, loss_parts = lax.map(block_terms, (values, a_rows, b_rows, c_rows, flags))

time: 562 us -> 543 us (0.966)
  waiting for transfers between devices: 233 us -> 201 us
  starting transfers between devices: 0.12 us -> 11.7 us
    all_gather x1 -> x0, waiting for transfers between devices: 66 us -> none  [per_device(): a_panel = lax.all_gather(factor_a, 'wide', axis=0, tiled=True)]
    all_to_all x0 -> x1, waiting for transfers between devices: none -> 34.7 us  [per_device(): jax.lax.all_to_all(jnp.stack(jax.lax.axis_size('wide') * [factor_a]), spl...]
    all_to_all x0 -> x1, starting transfers between devices: none -> 11.6 us  [per_device(): jax.lax.all_to_all(jnp.stack(jax.lax.axis_size('wide') * [factor_a]), spl...]
where the time goes in v1:
time: 543 us; the launch traced here: 540 us
  waiting for transfers between devices  201 us (37%)
  matrix products  115 us (21%)
  blocking collectives  88.2 us (16%)
  local copies, waits for them, and re-layouts  54.4 us (10%)
  loops' own time  27.7 us (5%)
  other arithmetic  24.8 us (5%)
  between operations  16.7 us (3%)
  starting transfers between devices  11.7 us (2%)
    reduce_scatter x1, waiting for transfers between devices, per_device(): lax.psum_scatter(panel_grad.reshape(panel_blocks * side, width), 'wide',...  166 us
    psum x1, blocking collectives, per_device(): lax.psum((jnp.sum(loss_parts), jnp.sum(flags)), ('grid', 'wide'))  74.9 us
    dot_general x14, matrix products, block_terms(): lax.dot_general(a_rows, khatri, (((1,), (1,)), ((), ())), preferred_eleme...  46.2 us
    dot_general x14, matrix products, block_terms(): grad_rows = jnp.dot(resid, khatri, preferred_element_type=jnp.float32)  37.5 us
    all_to_all x1, waiting for transfers between devices, per_device(): jax.lax.all_to_all(jnp.stack(jax.lax.axis_size('wide') * [factor_a]), spl...  34.7 us
    another operation x1, loops' own time, per_device(): lax.map(block_terms, (values, a_rows, b_rows, c_rows, flags))  27.7 us
    dot_general x14, matrix products, block_terms(): lax.dot_general(resid, a_rows, (((0,), (0,)), ((), ())), preferred_elemen...  26.9 us
    dot_general x14, local copies, waits for them, and re-layouts, block_terms(): lax.dot_general(resid, a_rows, (((0,), (0,)), ((), ())), preferred_elemen...  18.7 us
  transfers between devices with their start and end apart: 3, of which 2 were waited for; matrix products, arithmetic and copies ran while one was open for 3% of the time, Pallas kernels for 0%

profile of v1, /device:TPU:8, one launch (start us, length us, event | category | flops | bytes accessed | tf_op | source)
XLA Modules:
  0.0 539.9 jit_solution(7554224967395443461)
XLA Ops:
  7.2 2.5 stack.2
  9.7 11.6 %all-to-all-start = ((bf16[32,128,256]{2,1,0:T(8,128)(2,1)}), bf16[32,128,256]{2,1,0:T(8,128)(2,1)}, u32[]{:S(2)}, u32[]{:S(2)}) async-start(bf16[32,128,256]{2,1,0:T(8,128)(2,1)} %stack.2), calls=%async_computation | async-start | bytes 4194304 | tf_op jit(solution)/shard_map/all_to_all | solution.py:44
  22.1 13.3 %all_gather.3 = bf16[1024,256]{1,0:T(8,128)(2,1)S(1)} all-gather(bf16[128,256]{1,0:T(8,128)(2,1)S(1)} %copy-done.2), channel_id=1, replica_groups=mesh['grid'=8,'wide'=32] {'grid'}, dimensions={0}, use_global_device_ids=true | all-gather | bytes 589824 | tf_op jit(solution)/shard_map/all_gather | solution.py:40
  36.8 34.7 %all-to-all-done = bf16[32,128,256]{2,1,0:T(8,128)(2,1)} async-done(((bf16[32,128,256]{2,1,0:T(8,128)(2,1)}), bf16[32,128,256]{2,1,0:T(8,128)(2,1)}, u32[]{:S(2)}, u32[]{:S(2)}) %all-to-all-start) | async-done | bytes 2097184 | tf_op jit(solution)/shard_map/all_to_all | solution.py:44
  71.4 2.9 gather_fusion
  74.4 195.8 %while.14 = (s32[]{:T(128)}, f32[14,64,256]{2,1,0:T(8,128)}, f32[14,64,256]{2,1,0:T(8,128)}, f32[14]{0:T(128)S(1)}, bf16[14,64,256]{2,1,0:T(8,128)(2,1)}, /*inde...) while((s32[]{:T(128)}, f32[14,64,256]{2,1,0:T(8,128)}, ...), condition=%wide.region_3.4_spmd, body=%wide.region_0.3_spmd.sunk | while | flops 411058176 | bytes 19072724 | solution.py:54
  77.1 3.3 fusion.34
  81.7 2.7 fusion.35
  85.8 1.9 multiply_reduce_fusion.2
  91.1 3.3 fusion.34
  95.7 2.7 fusion.35
  99.8 1.9 multiply_reduce_fusion.2
  105.1 3.3 fusion.34
  109.7 2.7 fusion.35
  113.8 1.9 multiply_reduce_fusion.2
  119.1 3.3 fusion.34
  123.7 2.7 fusion.35
  127.8 1.9 multiply_reduce_fusion.2
  133.1 3.3 fusion.34
  137.7 2.7 fusion.35
  141.8 1.9 multiply_reduce_fusion.2
  147.0 3.3 fusion.34
  151.7 2.7 fusion.35
  155.8 1.9 multiply_reduce_fusion.2
  161.0 3.3 fusion.34
  165.6 2.7 fusion.35
  175.0 3.3 fusion.34
  179.6 2.7 fusion.35
  183.7 1.9 multiply_reduce_fusion.2
  189.0 3.3 fusion.34
  193.6 2.7 fusion.35
  203.0 3.3 fusion.34
  207.6 2.7 fusion.35
  211.7 1.9 multiply_reduce_fusion.2
  217.0 3.3 fusion.34
  221.6 2.7 fusion.35
  231.0 3.3 fusion.34
  235.6 2.7 fusion.35
  239.7 1.9 multiply_reduce_fusion.2
  245.0 3.3 fusion.34
  249.6 2.7 fusion.35
  258.9 3.3 fusion.34
  263.6 2.7 fusion.35
  267.7 1.9 multiply_reduce_fusion.2
  276.0 3.9 fusion.12
  279.9 4.9 reshape.57
  286.1 74.9 %all-reduce = (f32[]{:T(128)}, f32[]{:T(128)}) all-reduce(f32[]{:T(128)} %reduce_sum.36, f32[]{:T(128)} %convert_reduce_fusion), channel_id=1, replica_groups=mesh['grid'=8,'wide'=32] {'grid','wide'}, use_global_device_ids=true, to_apply=%region_7.8 | all-reduce | flops 2 | bytes 16 | tf_op jit(solution)/shard_map/psum | solution.py:69
  363.9 166.5 %reduce-scatter.3.cloned.1.call-done = f32[128,256]{1,0:T(8,128)} async-done(((f32[4096,256]{1,0:T(8,128)}), f32[128,256]{1,0:T(8,128)}) %reduce-scatter.3.cloned.1.call-update) | async-done | bytes 131088 | tf_op jit(solution)/shard_map/reduce_scatter | solution.py:58
  (157 shorter events, 77.4 us)
Async XLA Ops:
  7.2 14.3 %copy-start = (bf16[4096,256]{1,0:T(8,128)(2,1)S(1)}, bf16[4096,256]{1,0:T(8,128)(2,1)}, u32[]{:S(2)}) copy-start(bf16[4096,256]{1,0:T(8,128)(2,1)} %param.17) | copy-start | bytes 6291460
  9.7 11.7 %copy-start.7 = (s32[14]{0:T(128)S(1)}, s32[14]{0:T(128)}, u32[]{:S(2)}) copy-start(s32[14]{0:T(128)} %param.14) | copy-start | bytes 172
  9.7 11.7 %copy-start.6 = (s32[14]{0:T(128)S(1)}, s32[14]{0:T(128)}, u32[]{:S(2)}) copy-start(s32[14]{0:T(128)} %param.13) | copy-start | bytes 172
  9.7 12.3 %copy-start.4 = (s32[14]{0:T(128)S(1)}, s32[14]{0:T(128)}, u32[]{:S(2)}) copy-start(s32[14]{0:T(128)} %param.12) | copy-start | bytes 172
  9.7 12.4 %copy-start.2 = (bf16[128,256]{1,0:T(8,128)(2,1)S(1)}, bf16[128,256]{1,0:T(8,128)(2,1)}, u32[]{:S(2)}) copy-start(bf16[128,256]{1,0:T(8,128)(2,1)} %param.16) | copy-start | bytes 196612
  9.7 61.7 %all-to-all-start = ((bf16[32,128,256]{2,1,0:T(8,128)(2,1)}), bf16[32,128,256]{2,1,0:T(8,128)(2,1)}, u32[]{:S(2)}, u32[]{:S(2)}) async-start(bf16[32,128,256]{2,1,0:T(8,128)(2,1)} %stack.2), calls=%async_computation | async-start | bytes 4194304 | tf_op jit(solution)/shard_map/all_to_all | solution.py:44
  21.3 15.5 %copy-start.5 = (s32[14]{0:T(128)S(1)}, s32[14]{0:T(128)}, u32[]{:S(2)}) copy-start(s32[14]{0:T(128)} %param.11) | copy-start | bytes 172
  21.3 341.0 %reduce-scatter.5.cloned.1.call-start = ((), (), s32[]{:S(2)}) async-start(), calls=%async_computation.4 | async-start | bytes 1179648 | tf_op jit(solution)/shard_map/reduce_scatter | solution.py:66
  77.1 3.3 copy-start.1
  91.1 3.3 copy-start.1
  105.1 3.3 copy-start.1
  119.1 3.3 copy-start.1
  133.1 3.3 copy-start.1
  147.0 3.3 copy-start.1
  161.0 3.3 copy-start.1
  175.0 3.3 copy-start.1
  189.0 3.3 copy-start.1
  203.0 3.3 copy-start.1
  217.0 3.3 copy-start.1
  231.0 3.3 copy-start.1
  245.0 3.3 copy-start.1
  258.9 3.3 copy-start.1
  274.1 256.3 %reduce-scatter.3.cloned.1.call-start = ((), (), s32[]{:S(2)}) async-start(), calls=%async_computation.3 | async-start | bytes 4325376 | tf_op jit(solution)/shard_map/reduce_scatter | solution.py:58
  284.8 245.5 %copy-start.3 = (bf16[128,256]{1,0:T(8,128)(2,1)S(1)}, bf16[128,256]{1,0:T(8,128)(2,1)}, u32[]{:S(2)}) copy-start(bf16[128,256]{1,0:T(8,128)(2,1)} %param.15) | copy-start | bytes 196612
Sparse Core Ops, SparseCore 0:
  274.2 28.8 reduce-scatter.4
  307.0 223.3 reduce-scatter.2
